TPU v7x, 32 devices: a whole 2x2x4 slice. The times are simulated.
32 devices in a mesh: section: 4 (over x, core), obs: 8 (over z, y).
Axes of the slice: x: 2, y: 2, z: 4, core: 2. Of those that a mesh axis runs over, the one named last changes fastest.
Arguments:
- predictors: bfloat16 [4, 4, 20, 32768], P('section', None, None, 'obs'), may hold values from -5 to 5
- departures: float32 [4, 4, 32768], P('section', None, 'obs'), may hold values from -30 to 30
- obs_precision: float32 [4, 4, 32768], P('section', None, 'obs'), may hold values from 0.3 to 3
- qc_pass: int32 [4, 4, 32768], P('section', None, 'obs'), may hold values 0 or 1
- block_channel: int32 [4, 4, 256], P('section', None, 'obs'), may hold values from 0 to 2047, as said below
- stream_order: int32 [4], replicated, may hold values from 0 to 3, each once
- prior_coeffs: float32 [4, 20, 2048], P(None, None, 'obs'), may hold values from -1 to 1
- prior_info: float32 [4, 210, 2048], P(None, None, 'obs'), may hold values from -1 to 32, as said below
- memory_factor: float32 [2048], P('obs'), may hold values from 0.5 to 0.98
Outputs:
- coeffs: float32 [4, 4, 20, 2048], P('section', None, None, 'obs')
- information: float32 [4, 4, 210, 2048], P('section', None, None, 'obs')
Inputs may be any that keep to these rules, and one draw needn't show every extreme that they name: `block_channel`: among the 32 row blocks of one index of obs, at most 8 have channels in any one range of the 256 channels from a multiple of 256; in every window and stream one such range holds exactly 8 blocks of every index of obs. `stream_order`: each stream appears once. `prior_info`: for every stream and channel the 210 entries are the upper triangle, row by row, of a symmetric positive definite matrix of order 20.
All inputs are finite; a program needn't handle non-finite values. No bound on the sum of `qc_pass` on one device may be relied on, other than what follows from the above.
Results may differ from a plain program's by a relative error of at most 0.0038.
Values sent between devices are 32-bit elements; how exact they have to be, the bound alone decides.
A program may use at most 64 MiB of HBM per device.

v0:
```python
import jax
import jax.numpy as jnp
import numpy as np
from jax import lax
from jax.sharding import PartitionSpec as P

HUBER_SQ = 9.0
PRIOR_WEIGHT = 64.0


def from_behind(array, axis, by):
    size = lax.axis_size(axis)
    pairs = [(i, i + by) for i in range(size) if 0 <= i + by < size]
    return lax.ppermute(array, axis, pairs)


def upper_positions(dimension):
    return np.array(
        [i * dimension + j for i in range(dimension) for j in range(i, dimension)], dtype=np.int32
    )


def solve_packed(packed, target):
    dimension = target.shape[0]
    placing = {}
    counter = 0
    for i in range(dimension):
        for j in range(i, dimension):
            placing[i, j] = counter
            counter += 1
    factor = [[None] * dimension for i in range(dimension)]
    for j in range(dimension):
        pivot_root = jnp.sqrt(
            packed[placing[j, j]] - sum((factor[j][k] * factor[j][k] for k in range(j)))
        )
        factor[j][j] = pivot_root
        for i in range(j + 1, dimension):
            factor[i][j] = (
                packed[placing[j, i]] - sum((factor[i][k] * factor[j][k] for k in range(j)))
            ) / pivot_root
    forward = []
    for i in range(dimension):
        forward.append(
            (target[i] - sum((factor[i][k] * forward[k] for k in range(i)))) / factor[i][i]
        )
    backward = [None] * dimension
    for i in reversed(range(dimension)):
        backward[i] = (
            forward[i] - sum((factor[k][i] * backward[k] for k in range(i + 1, dimension)))
        ) / factor[i][i]
    return jnp.stack(backward)


def block_terms(predicted, departed, precision, passed, block_coeffs):
    pred_count, row_count = predicted.shape
    block_count = block_coeffs.shape[1]
    block_width = row_count // block_count
    upper_index = upper_positions(pred_count)
    shaped = predicted.reshape(pred_count, block_count, block_width)
    offset = jnp.sum(shaped.astype(jnp.float32) * block_coeffs[:, :, None], axis=0)
    residual = departed.reshape(block_count, block_width) - offset
    scale_row = precision.reshape(block_count, block_width)
    weight = (
        passed.reshape(block_count, block_width).astype(jnp.float32)
        * scale_row
        / (1.0 + scale_row * residual * residual / HUBER_SQ)
    )
    weighted = (weight[None] * shaped.astype(jnp.float32)).astype(jnp.bfloat16)
    chi_square = jnp.sum(weight * residual * residual)
    passed_count = jnp.sum(passed.astype(jnp.float32))
    gram_full = lax.dot_general(
        weighted, shaped, (((2,), (2,)), ((1,), (1,))), preferred_element_type=jnp.float32
    )
    gram_upper = gram_full.reshape(block_count, pred_count * pred_count)[:, upper_index]
    gradient = jnp.sum(weighted.astype(jnp.float32) * residual[None], axis=2).T
    return (jnp.concatenate([gram_upper, gradient], axis=1), jnp.stack([chi_square, passed_count]))


def local(
    predictors,
    departures,
    obs_precision,
    qc_pass,
    block_channel,
    stream_order,
    prior_coeffs,
    prior_info,
    memory_factor,
):
    section_count = lax.axis_size("section")
    obs_devices = lax.axis_size("obs")
    section_place = lax.axis_index("section")
    stream_count = stream_order.shape[0]
    local_channels = memory_factor.shape[0]
    block_count = block_channel.shape[2]
    pred_count = prior_coeffs.shape[1]
    tri_count = prior_info.shape[1]
    column_count = tri_count + pred_count
    capacity = 2 * block_count // obs_devices
    local_line = jnp.arange(local_channels, dtype=jnp.float32)
    owner_line = jnp.arange(obs_devices, dtype=jnp.int32)
    slot_line = jnp.arange(obs_devices * capacity, dtype=jnp.int32)
    highest = lax.Precision.HIGHEST

    def pack_blocks(block_sums, channel):
        owner_index = channel // local_channels
        inner_channel = channel % local_channels
        owner_hot = (owner_index[:, None] == owner_line[None, :]).astype(jnp.int32)
        ranking = jnp.sum((jnp.cumsum(owner_hot, axis=0) - 1) * owner_hot, axis=1)
        slot_of = owner_index * capacity + ranking
        placing = (slot_of[:, None] == slot_line[None, :]).astype(jnp.float32)
        send_rows = lax.dot_general(
            placing,
            block_sums,
            (((0,), (0,)), ((), ())),
            precision=highest,
            preferred_element_type=jnp.float32,
        ).reshape(obs_devices, capacity, column_count)
        send_channel = (
            lax.dot_general(
                placing,
                (inner_channel + 1).astype(jnp.float32),
                (((0,), (0,)), ((), ())),
                precision=highest,
                preferred_element_type=jnp.float32,
            ).reshape(obs_devices, capacity)
            - 1.0
        )
        return (send_rows, send_channel)

    def unpack_blocks(got_rows, got_channel):
        gather_hot = (got_channel.reshape(-1)[:, None] == local_line[None, :]).astype(jnp.float32)
        return lax.dot_general(
            got_rows.reshape(-1, column_count),
            gather_hot,
            (((0,), (0,)), ((), ())),
            precision=highest,
            preferred_element_type=jnp.float32,
        )

    def window_work(state_now, streams):
        beta_prior = state_now[:, :pred_count]
        info_prior = state_now[:, pred_count:]
        all_coeffs = lax.all_gather(beta_prior, "obs", axis=2, tiled=True)
        channel = jnp.take(block_channel[0], streams, axis=0)
        block_coeffs = jax.vmap(lambda coeff_rows, chan: jnp.take(coeff_rows, chan, axis=1))(
            all_coeffs, channel
        )
        block_sums, statistics = jax.vmap(block_terms)(
            jnp.take(predictors[0], streams, axis=0),
            jnp.take(departures[0], streams, axis=0),
            jnp.take(obs_precision[0], streams, axis=0),
            jnp.take(qc_pass[0], streams, axis=0),
            block_coeffs,
        )
        totals = lax.psum(statistics, "obs")
        send_rows, send_channel = jax.vmap(pack_blocks)(block_sums, channel)
        got_rows, got_channel = (
            lax.all_to_all(send_rows, "obs", split_axis=1, concat_axis=1, tiled=True),
            lax.all_to_all(send_channel, "obs", split_axis=1, concat_axis=1, tiled=True),
        )
        normal = jax.vmap(unpack_blocks)(got_rows, got_channel)
        inflation = (totals[:, 0] + PRIOR_WEIGHT) / (totals[:, 1] + PRIOR_WEIGHT)
        info_post = info_prior + normal[:, :tri_count] / inflation[:, None, None]
        beta_post = beta_prior + jax.vmap(solve_packed)(
            info_post, normal[:, tri_count:] / inflation[:, None, None]
        )
        outgoing = jnp.concatenate([beta_post, memory_factor[None, None, :] * info_post], axis=1)
        incoming = from_behind(outgoing, "section", 1)
        return (beta_post, info_post, incoming)

    def fresh_of(streams):
        return jnp.concatenate(
            [jnp.take(prior_coeffs, streams, axis=0), jnp.take(prior_info, streams, axis=0)], axis=1
        )

    coeff_start = jnp.zeros((1, stream_count, pred_count, local_channels), jnp.float32)
    info_start = jnp.zeros((1, stream_count, tri_count, local_channels), jnp.float32)

    def tick_step(t, loop_state):
        incoming, coeff_out, info_out = loop_state
        entry_index = t - section_place
        usable = (entry_index >= 0) & (entry_index < stream_count)
        slot_index = jnp.clip(entry_index, 0, stream_count - 1)
        streams = lax.dynamic_slice_in_dim(stream_order, slot_index, 1, 0)
        state_now = jnp.where(
            (section_place == 0) | jnp.logical_not(usable), fresh_of(streams), incoming
        )
        beta_post, info_post, incoming = window_work(state_now, streams)

        def store_entry(buffer, result):
            current = lax.dynamic_slice_in_dim(buffer, slot_index, 1, 1)
            updated = jnp.where(usable, result[None], current)
            return lax.dynamic_update_slice_in_dim(buffer, updated, slot_index, 1)

        return (incoming, store_entry(coeff_out, beta_post), store_entry(info_out, info_post))

    initial = (jnp.zeros((1, column_count, local_channels), jnp.float32), coeff_start, info_start)
    final_state = lax.fori_loop(0, stream_count + section_count - 1, tick_step, initial)
    return (final_state[1], final_state[2])


def solution(mesh):
    in_specs = (
        P("section", None, None, "obs"),
        P("section", None, "obs"),
        P("section", None, "obs"),
        P("section", None, "obs"),
        P("section", None, "obs"),
        P(),
        P(None, None, "obs"),
        P(None, None, "obs"),
        P("obs"),
    )
    out_specs = (P("section", None, None, "obs"), P("section", None, None, "obs"))
    return jax.shard_map(local, mesh=mesh, in_specs=in_specs, out_specs=out_specs, check_vma=False)
```

profile of v0, /device:TPU:1, one launch (start us, length us, event | category | flops | bytes accessed | tf_op | source)
XLA Modules:
  0.0 688.5 jit_solution(5905409147109336993)
XLA Ops:
  0.6 1.5 copy.675
  2.9 684.6 %while.38 = (s32[]{:T(128)}, f32[1,230,256]{2,1,0:T(8,128)S(1)}, f32[1,4,20,256]{3,1,2,0:T(4,128)S(1)}, f32[1,4,210,256]{3,1,2,0:T(4,128)S(1)}, s32[]{:T(128)}, ...) while((s32[]{:T(128)}, f32[1,230,256]{2,1,0:T(8,128)S(1)}, ...), condition=%wide.region_8.10_spmd.clone.clone, body=%wide.region_0.9_spmd.sunk.clone.clone.sunk | while | flops 57759508 | bytes 13853709 | solution.py:199
  7.5 6.4 all-to-all-start.1
  13.9 1.4 constant_dynamic-slice_fusion.10
  16.3 24.6 %all_gather.15 = f32[1,20,2048]{2,1,0:T(8,128)S(1)} all-gather(f32[1,20,256]{2,1,0:T(8,128)S(1)} %slice.5342), channel_id=1, replica_groups=mesh['section'=4,'obs'=8] {'obs'}, dimensions={2}, use_global_device_ids=true | all-gather | bytes 184320 | tf_op jit(solution)/shard_map/while/body/eval_jaxpr/all_gather | solution.py:144
  42.3 1.6 fusion.473
  47.6 17.5 %psum.19 = f32[1,2]{1,0:T(1,128)S(1)} all-reduce(f32[1,2]{1,0:T(1,128)S(1)} %maximum_bitcast_fusion.6), channel_id=1, replica_groups=mesh['section'=4,'obs'=8] {'obs'}, use_global_device_ids=true, to_apply=%region_7.8 | all-reduce | flops 2 | bytes 16 | tf_op jit(solution)/shard_map/while/body/eval_jaxpr/psum | solution.py:156
  68.0 3.4 all-to-all-start
  72.6 4.4 all-to-all-done
  83.2 15.7 %collective-permute-start = (f32[1,230,256]{2,1,0:T(8,128)S(1)}, f32[1,230,256]{2,1,0:T(8,128)S(1)}, u32[]{:S(2)}, u32[]{:S(2)}) collective-permute-start(f32[1,230,256]{2,1,0:T(8,128)S(1)} %pad_maximum_fusion.2), channel_id=1, source_target_pairs={{0,8},{8,16},{16,24},{1,9},{9,17},{17,25},{2,10},{10,18},{18,26},{... | collective-permute-start | bytes 706568 | tf_op jit(solution)/shard_map/while/body/eval_jaxpr/ppermute | solution.py:14
  99.3 5.9 dynamic_update_slice.31
  109.8 3.3 all-to-all-start.1
  113.2 1.4 constant_dynamic-slice_fusion.10
  115.6 25.2 %all_gather.15 = f32[1,20,2048]{2,1,0:T(8,128)S(1)} all-gather(f32[1,20,256]{2,1,0:T(8,128)S(1)} %slice.5342), channel_id=1, replica_groups=mesh['section'=4,'obs'=8] {'obs'}, dimensions={2}, use_global_device_ids=true | all-gather | bytes 184320 | tf_op jit(solution)/shard_map/while/body/eval_jaxpr/all_gather | solution.py:144
  142.2 1.6 fusion.473
  147.5 17.3 %psum.19 = f32[1,2]{1,0:T(1,128)S(1)} all-reduce(f32[1,2]{1,0:T(1,128)S(1)} %maximum_bitcast_fusion.6), channel_id=1, replica_groups=mesh['section'=4,'obs'=8] {'obs'}, use_global_device_ids=true, to_apply=%region_7.8 | all-reduce | flops 2 | bytes 16 | tf_op jit(solution)/shard_map/while/body/eval_jaxpr/psum | solution.py:156
  167.6 3.4 all-to-all-start
  172.3 4.4 all-to-all-done
  182.9 13.1 %collective-permute-start = (f32[1,230,256]{2,1,0:T(8,128)S(1)}, f32[1,230,256]{2,1,0:T(8,128)S(1)}, u32[]{:S(2)}, u32[]{:S(2)}) collective-permute-start(f32[1,230,256]{2,1,0:T(8,128)S(1)} %pad_maximum_fusion.2), channel_id=1, source_target_pairs={{0,8},{8,16},{16,24},{1,9},{9,17},{17,25},{2,10},{10,18},{18,26},{... | collective-permute-start | bytes 706568 | tf_op jit(solution)/shard_map/while/body/eval_jaxpr/ppermute | solution.py:14
  196.4 5.9 dynamic_update_slice.31
  206.9 3.3 all-to-all-start.1
  210.2 1.4 constant_dynamic-slice_fusion.10
  212.6 24.6 %all_gather.15 = f32[1,20,2048]{2,1,0:T(8,128)S(1)} all-gather(f32[1,20,256]{2,1,0:T(8,128)S(1)} %slice.5342), channel_id=1, replica_groups=mesh['section'=4,'obs'=8] {'obs'}, dimensions={2}, use_global_device_ids=true | all-gather | bytes 184320 | tf_op jit(solution)/shard_map/while/body/eval_jaxpr/all_gather | solution.py:144
  238.7 1.6 fusion.473
  244.0 17.5 %psum.19 = f32[1,2]{1,0:T(1,128)S(1)} all-reduce(f32[1,2]{1,0:T(1,128)S(1)} %maximum_bitcast_fusion.6), channel_id=1, replica_groups=mesh['section'=4,'obs'=8] {'obs'}, use_global_device_ids=true, to_apply=%region_7.8 | all-reduce | flops 2 | bytes 16 | tf_op jit(solution)/shard_map/while/body/eval_jaxpr/psum | solution.py:156
  264.4 3.4 all-to-all-start
  269.0 4.4 all-to-all-done
  279.6 13.4 %collective-permute-start = (f32[1,230,256]{2,1,0:T(8,128)S(1)}, f32[1,230,256]{2,1,0:T(8,128)S(1)}, u32[]{:S(2)}, u32[]{:S(2)}) collective-permute-start(f32[1,230,256]{2,1,0:T(8,128)S(1)} %pad_maximum_fusion.2), channel_id=1, source_target_pairs={{0,8},{8,16},{16,24},{1,9},{9,17},{17,25},{2,10},{10,18},{18,26},{... | collective-permute-start | bytes 706568 | tf_op jit(solution)/shard_map/while/body/eval_jaxpr/ppermute | solution.py:14
  293.4 5.9 dynamic_update_slice.31
  303.9 3.3 all-to-all-start.1
  307.3 1.4 constant_dynamic-slice_fusion.10
  309.7 24.8 %all_gather.15 = f32[1,20,2048]{2,1,0:T(8,128)S(1)} all-gather(f32[1,20,256]{2,1,0:T(8,128)S(1)} %slice.5342), channel_id=1, replica_groups=mesh['section'=4,'obs'=8] {'obs'}, dimensions={2}, use_global_device_ids=true | all-gather | bytes 184320 | tf_op jit(solution)/shard_map/while/body/eval_jaxpr/all_gather | solution.py:144
  336.0 1.6 fusion.473
  341.3 17.6 %psum.19 = f32[1,2]{1,0:T(1,128)S(1)} all-reduce(f32[1,2]{1,0:T(1,128)S(1)} %maximum_bitcast_fusion.6), channel_id=1, replica_groups=mesh['section'=4,'obs'=8] {'obs'}, use_global_device_ids=true, to_apply=%region_7.8 | all-reduce | flops 2 | bytes 16 | tf_op jit(solution)/shard_map/while/body/eval_jaxpr/psum | solution.py:156
  361.8 3.4 all-to-all-start
  366.4 4.4 all-to-all-done
  377.0 13.1 %collective-permute-start = (f32[1,230,256]{2,1,0:T(8,128)S(1)}, f32[1,230,256]{2,1,0:T(8,128)S(1)}, u32[]{:S(2)}, u32[]{:S(2)}) collective-permute-start(f32[1,230,256]{2,1,0:T(8,128)S(1)} %pad_maximum_fusion.2), channel_id=1, source_target_pairs={{0,8},{8,16},{16,24},{1,9},{9,17},{17,25},{2,10},{10,18},{18,26},{... | collective-permute-start | bytes 706568 | tf_op jit(solution)/shard_map/while/body/eval_jaxpr/ppermute | solution.py:14
  390.5 5.9 dynamic_update_slice.31
  401.0 3.3 all-to-all-start.1
  406.7 24.9 %all_gather.15 = f32[1,20,2048]{2,1,0:T(8,128)S(1)} all-gather(f32[1,20,256]{2,1,0:T(8,128)S(1)} %slice.5342), channel_id=1, replica_groups=mesh['section'=4,'obs'=8] {'obs'}, dimensions={2}, use_global_device_ids=true | all-gather | bytes 184320 | tf_op jit(solution)/shard_map/while/body/eval_jaxpr/all_gather | solution.py:144
  433.2 1.6 fusion.473
  438.4 17.2 %psum.19 = f32[1,2]{1,0:T(1,128)S(1)} all-reduce(f32[1,2]{1,0:T(1,128)S(1)} %maximum_bitcast_fusion.6), channel_id=1, replica_groups=mesh['section'=4,'obs'=8] {'obs'}, use_global_device_ids=true, to_apply=%region_7.8 | all-reduce | flops 2 | bytes 16 | tf_op jit(solution)/shard_map/while/body/eval_jaxpr/psum | solution.py:156
  458.5 3.4 all-to-all-start
  463.2 4.4 all-to-all-done
  473.8 13.4 %collective-permute-start = (f32[1,230,256]{2,1,0:T(8,128)S(1)}, f32[1,230,256]{2,1,0:T(8,128)S(1)}, u32[]{:S(2)}, u32[]{:S(2)}) collective-permute-start(f32[1,230,256]{2,1,0:T(8,128)S(1)} %pad_maximum_fusion.2), channel_id=1, source_target_pairs={{0,8},{8,16},{16,24},{1,9},{9,17},{17,25},{2,10},{10,18},{18,26},{... | collective-permute-start | bytes 706568 | tf_op jit(solution)/shard_map/while/body/eval_jaxpr/ppermute | solution.py:14
  487.5 5.9 dynamic_update_slice.31
  498.1 3.3 all-to-all-start.1
  501.4 1.4 constant_dynamic-slice_fusion.10
  503.8 24.8 %all_gather.15 = f32[1,20,2048]{2,1,0:T(8,128)S(1)} all-gather(f32[1,20,256]{2,1,0:T(8,128)S(1)} %slice.5342), channel_id=1, replica_groups=mesh['section'=4,'obs'=8] {'obs'}, dimensions={2}, use_global_device_ids=true | all-gather | bytes 184320 | tf_op jit(solution)/shard_map/while/body/eval_jaxpr/all_gather | solution.py:144
  530.1 1.6 fusion.473
  535.4 17.5 %psum.19 = f32[1,2]{1,0:T(1,128)S(1)} all-reduce(f32[1,2]{1,0:T(1,128)S(1)} %maximum_bitcast_fusion.6), channel_id=1, replica_groups=mesh['section'=4,'obs'=8] {'obs'}, use_global_device_ids=true, to_apply=%region_7.8 | all-reduce | flops 2 | bytes 16 | tf_op jit(solution)/shard_map/while/body/eval_jaxpr/psum | solution.py:156
  555.8 3.4 all-to-all-start
  560.4 4.4 all-to-all-done
  571.0 13.2 %collective-permute-start = (f32[1,230,256]{2,1,0:T(8,128)S(1)}, f32[1,230,256]{2,1,0:T(8,128)S(1)}, u32[]{:S(2)}, u32[]{:S(2)}) collective-permute-start(f32[1,230,256]{2,1,0:T(8,128)S(1)} %pad_maximum_fusion.2), channel_id=1, source_target_pairs={{0,8},{8,16},{16,24},{1,9},{9,17},{17,25},{2,10},{10,18},{18,26},{... | collective-permute-start | bytes 706568 | tf_op jit(solution)/shard_map/while/body/eval_jaxpr/ppermute | solution.py:14
  584.6 5.9 dynamic_update_slice.31
  595.1 3.3 all-to-all-start.1
  598.5 1.4 constant_dynamic-slice_fusion.10
  600.9 24.5 %all_gather.15 = f32[1,20,2048]{2,1,0:T(8,128)S(1)} all-gather(f32[1,20,256]{2,1,0:T(8,128)S(1)} %slice.5342), channel_id=1, replica_groups=mesh['section'=4,'obs'=8] {'obs'}, dimensions={2}, use_global_device_ids=true | all-gather | bytes 184320 | tf_op jit(solution)/shard_map/while/body/eval_jaxpr/all_gather | solution.py:144
  626.8 1.6 fusion.473
  632.1 18.0 %psum.19 = f32[1,2]{1,0:T(1,128)S(1)} all-reduce(f32[1,2]{1,0:T(1,128)S(1)} %maximum_bitcast_fusion.6), channel_id=1, replica_groups=mesh['section'=4,'obs'=8] {'obs'}, use_global_device_ids=true, to_apply=%region_7.8 | all-reduce | flops 2 | bytes 16 | tf_op jit(solution)/shard_map/while/body/eval_jaxpr/psum | solution.py:156
  652.9 3.4 all-to-all-start
  657.6 4.4 all-to-all-done
  668.2 13.1 %collective-permute-start = (f32[1,230,256]{2,1,0:T(8,128)S(1)}, f32[1,230,256]{2,1,0:T(8,128)S(1)}, u32[]{:S(2)}, u32[]{:S(2)}) collective-permute-start(f32[1,230,256]{2,1,0:T(8,128)S(1)} %pad_maximum_fusion.2), channel_id=1, source_target_pairs={{0,8},{8,16},{16,24},{1,9},{9,17},{17,25},{2,10},{10,18},{18,26},{... | collective-permute-start | bytes 706568 | tf_op jit(solution)/shard_map/while/body/eval_jaxpr/ppermute | solution.py:14
  681.7 5.9 dynamic_update_slice.31
  (616 shorter events, 128.2 us)
Async XLA Ops:
  2.2 0.7 copy-start.4
  2.3 0.7 copy-start.5
  2.3 0.7 copy-start.6
  7.5 60.4 %all-to-all-start.1 = ((f32[1,8,8]{2,0,1:T(1,128)}), f32[1,8,8]{2,0,1:T(1,128)S(1)}, u32[]{:S(2)}, u32[]{:S(2)}) async-start(f32[1,8,8]{2,0,1:T(1,128)} %bitcast.2454), calls=%async_computation.1 | async-start | bytes 8192 | tf_op jit(solution)/shard_map/while/body/eval_jaxpr/all_to_all | solution.py:160
  68.0 9.1 %all-to-all-start = ((f32[1,8,8,230]{3,2,0,1:T(8,128)}), f32[1,8,8,230]{3,2,0,1:T(8,128)S(1)}, u32[]{:S(2)}, u32[]{:S(2)}) async-start(f32[1,8,8,230]{3,2,0,1:T(8,128)} %convolution_bitcast_fusion.4), calls=%async_computation | async-start | bytes 131072 | tf_op jit(solution)/shard_map/while/body/eval_jaxpr/all_to_all | solution.py:159
  77.4 0.6 copy-start
  78.8 0.7 slice-start
  80.7 0.7 copy-start.1
  83.2 22.0 %collective-permute-start = (f32[1,230,256]{2,1,0:T(8,128)S(1)}, f32[1,230,256]{2,1,0:T(8,128)S(1)}, u32[]{:S(2)}, u32[]{:S(2)}) collective-permute-start(f32[1,230,256]{2,1,0:T(8,128)S(1)} %pad_maximum_fusion.2), channel_id=1, source_target_pairs={{0,8},{8,16},{16,24},{1,9},{9,17},{17,25},{2,10},{10,18},{18,26},{... | collective-permute-start | bytes 706568 | tf_op jit(solution)/shard_map/while/body/eval_jaxpr/ppermute | solution.py:14
  109.8 57.8 %all-to-all-start.1 = ((f32[1,8,8]{2,0,1:T(1,128)}), f32[1,8,8]{2,0,1:T(1,128)S(1)}, u32[]{:S(2)}, u32[]{:S(2)}) async-start(f32[1,8,8]{2,0,1:T(1,128)} %bitcast.2454), calls=%async_computation.1 | async-start | bytes 8192 | tf_op jit(solution)/shard_map/while/body/eval_jaxpr/all_to_all | solution.py:160
  167.6 9.1 %all-to-all-start = ((f32[1,8,8,230]{3,2,0,1:T(8,128)}), f32[1,8,8,230]{3,2,0,1:T(8,128)S(1)}, u32[]{:S(2)}, u32[]{:S(2)}) async-start(f32[1,8,8,230]{3,2,0,1:T(8,128)} %convolution_bitcast_fusion.4), calls=%async_computation | async-start | bytes 131072 | tf_op jit(solution)/shard_map/while/body/eval_jaxpr/all_to_all | solution.py:159
  177.1 0.6 copy-start
  178.5 0.7 slice-start
  180.4 0.7 copy-start.1
  182.9 19.4 %collective-permute-start = (f32[1,230,256]{2,1,0:T(8,128)S(1)}, f32[1,230,256]{2,1,0:T(8,128)S(1)}, u32[]{:S(2)}, u32[]{:S(2)}) collective-permute-start(f32[1,230,256]{2,1,0:T(8,128)S(1)} %pad_maximum_fusion.2), channel_id=1, source_target_pairs={{0,8},{8,16},{16,24},{1,9},{9,17},{17,25},{2,10},{10,18},{18,26},{... | collective-permute-start | bytes 706568 | tf_op jit(solution)/shard_map/while/body/eval_jaxpr/ppermute | solution.py:14
  206.9 57.5 %all-to-all-start.1 = ((f32[1,8,8]{2,0,1:T(1,128)}), f32[1,8,8]{2,0,1:T(1,128)S(1)}, u32[]{:S(2)}, u32[]{:S(2)}) async-start(f32[1,8,8]{2,0,1:T(1,128)} %bitcast.2454), calls=%async_computation.1 | async-start | bytes 8192 | tf_op jit(solution)/shard_map/while/body/eval_jaxpr/all_to_all | solution.py:160
  264.4 9.1 %all-to-all-start = ((f32[1,8,8,230]{3,2,0,1:T(8,128)}), f32[1,8,8,230]{3,2,0,1:T(8,128)S(1)}, u32[]{:S(2)}, u32[]{:S(2)}) async-start(f32[1,8,8,230]{3,2,0,1:T(8,128)} %convolution_bitcast_fusion.4), calls=%async_computation | async-start | bytes 131072 | tf_op jit(solution)/shard_map/while/body/eval_jaxpr/all_to_all | solution.py:159
  273.8 0.6 copy-start
  275.2 0.7 slice-start
  277.1 0.7 copy-start.1
  279.6 19.7 %collective-permute-start = (f32[1,230,256]{2,1,0:T(8,128)S(1)}, f32[1,230,256]{2,1,0:T(8,128)S(1)}, u32[]{:S(2)}, u32[]{:S(2)}) collective-permute-start(f32[1,230,256]{2,1,0:T(8,128)S(1)} %pad_maximum_fusion.2), channel_id=1, source_target_pairs={{0,8},{8,16},{16,24},{1,9},{9,17},{17,25},{2,10},{10,18},{18,26},{... | collective-permute-start | bytes 706568 | tf_op jit(solution)/shard_map/while/body/eval_jaxpr/ppermute | solution.py:14
  303.9 57.8 %all-to-all-start.1 = ((f32[1,8,8]{2,0,1:T(1,128)}), f32[1,8,8]{2,0,1:T(1,128)S(1)}, u32[]{:S(2)}, u32[]{:S(2)}) async-start(f32[1,8,8]{2,0,1:T(1,128)} %bitcast.2454), calls=%async_computation.1 | async-start | bytes 8192 | tf_op jit(solution)/shard_map/while/body/eval_jaxpr/all_to_all | solution.py:160
  361.8 9.1 %all-to-all-start = ((f32[1,8,8,230]{3,2,0,1:T(8,128)}), f32[1,8,8,230]{3,2,0,1:T(8,128)S(1)}, u32[]{:S(2)}, u32[]{:S(2)}) async-start(f32[1,8,8,230]{3,2,0,1:T(8,128)} %convolution_bitcast_fusion.4), calls=%async_computation | async-start | bytes 131072 | tf_op jit(solution)/shard_map/while/body/eval_jaxpr/all_to_all | solution.py:159
  371.2 0.6 copy-start
  372.6 0.7 slice-start
  374.5 0.7 copy-start.1
  377.0 19.4 %collective-permute-start = (f32[1,230,256]{2,1,0:T(8,128)S(1)}, f32[1,230,256]{2,1,0:T(8,128)S(1)}, u32[]{:S(2)}, u32[]{:S(2)}) collective-permute-start(f32[1,230,256]{2,1,0:T(8,128)S(1)} %pad_maximum_fusion.2), channel_id=1, source_target_pairs={{0,8},{8,16},{16,24},{1,9},{9,17},{17,25},{2,10},{10,18},{18,26},{... | collective-permute-start | bytes 706568 | tf_op jit(solution)/shard_map/while/body/eval_jaxpr/ppermute | solution.py:14
  401.0 57.5 %all-to-all-start.1 = ((f32[1,8,8]{2,0,1:T(1,128)}), f32[1,8,8]{2,0,1:T(1,128)S(1)}, u32[]{:S(2)}, u32[]{:S(2)}) async-start(f32[1,8,8]{2,0,1:T(1,128)} %bitcast.2454), calls=%async_computation.1 | async-start | bytes 8192 | tf_op jit(solution)/shard_map/while/body/eval_jaxpr/all_to_all | solution.py:160
  458.5 9.1 %all-to-all-start = ((f32[1,8,8,230]{3,2,0,1:T(8,128)}), f32[1,8,8,230]{3,2,0,1:T(8,128)S(1)}, u32[]{:S(2)}, u32[]{:S(2)}) async-start(f32[1,8,8,230]{3,2,0,1:T(8,128)} %convolution_bitcast_fusion.4), calls=%async_computation | async-start | bytes 131072 | tf_op jit(solution)/shard_map/while/body/eval_jaxpr/all_to_all | solution.py:159
  468.0 0.6 copy-start
  469.4 0.7 slice-start
  471.3 0.7 copy-start.1
  473.8 19.7 %collective-permute-start = (f32[1,230,256]{2,1,0:T(8,128)S(1)}, f32[1,230,256]{2,1,0:T(8,128)S(1)}, u32[]{:S(2)}, u32[]{:S(2)}) collective-permute-start(f32[1,230,256]{2,1,0:T(8,128)S(1)} %pad_maximum_fusion.2), channel_id=1, source_target_pairs={{0,8},{8,16},{16,24},{1,9},{9,17},{17,25},{2,10},{10,18},{18,26},{... | collective-permute-start | bytes 706568 | tf_op jit(solution)/shard_map/while/body/eval_jaxpr/ppermute | solution.py:14
  498.1 57.7 %all-to-all-start.1 = ((f32[1,8,8]{2,0,1:T(1,128)}), f32[1,8,8]{2,0,1:T(1,128)S(1)}, u32[]{:S(2)}, u32[]{:S(2)}) async-start(f32[1,8,8]{2,0,1:T(1,128)} %bitcast.2454), calls=%async_computation.1 | async-start | bytes 8192 | tf_op jit(solution)/shard_map/while/body/eval_jaxpr/all_to_all | solution.py:160
  555.8 9.1 %all-to-all-start = ((f32[1,8,8,230]{3,2,0,1:T(8,128)}), f32[1,8,8,230]{3,2,0,1:T(8,128)S(1)}, u32[]{:S(2)}, u32[]{:S(2)}) async-start(f32[1,8,8,230]{3,2,0,1:T(8,128)} %convolution_bitcast_fusion.4), calls=%async_computation | async-start | bytes 131072 | tf_op jit(solution)/shard_map/while/body/eval_jaxpr/all_to_all | solution.py:159
  565.2 0.6 copy-start
  566.6 0.7 slice-start
  568.5 0.7 copy-start.1
  571.0 19.5 %collective-permute-start = (f32[1,230,256]{2,1,0:T(8,128)S(1)}, f32[1,230,256]{2,1,0:T(8,128)S(1)}, u32[]{:S(2)}, u32[]{:S(2)}) collective-permute-start(f32[1,230,256]{2,1,0:T(8,128)S(1)} %pad_maximum_fusion.2), channel_id=1, source_target_pairs={{0,8},{8,16},{16,24},{1,9},{9,17},{17,25},{2,10},{10,18},{18,26},{... | collective-permute-start | bytes 706568 | tf_op jit(solution)/shard_map/while/body/eval_jaxpr/ppermute | solution.py:14
  595.1 57.8 %all-to-all-start.1 = ((f32[1,8,8]{2,0,1:T(1,128)}), f32[1,8,8]{2,0,1:T(1,128)S(1)}, u32[]{:S(2)}, u32[]{:S(2)}) async-start(f32[1,8,8]{2,0,1:T(1,128)} %bitcast.2454), calls=%async_computation.1 | async-start | bytes 8192 | tf_op jit(solution)/shard_map/while/body/eval_jaxpr/all_to_all | solution.py:160
  652.9 9.1 %all-to-all-start = ((f32[1,8,8,230]{3,2,0,1:T(8,128)}), f32[1,8,8,230]{3,2,0,1:T(8,128)S(1)}, u32[]{:S(2)}, u32[]{:S(2)}) async-start(f32[1,8,8,230]{3,2,0,1:T(8,128)} %convolution_bitcast_fusion.4), calls=%async_computation | async-start | bytes 131072 | tf_op jit(solution)/shard_map/while/body/eval_jaxpr/all_to_all | solution.py:159
  662.4 0.6 copy-start
  663.8 0.7 slice-start
  665.7 0.7 copy-start.1
  668.2 19.4 %collective-permute-start = (f32[1,230,256]{2,1,0:T(8,128)S(1)}, f32[1,230,256]{2,1,0:T(8,128)S(1)}, u32[]{:S(2)}, u32[]{:S(2)}) collective-permute-start(f32[1,230,256]{2,1,0:T(8,128)S(1)} %pad_maximum_fusion.2), channel_id=1, source_target_pairs={{0,8},{8,16},{16,24},{1,9},{9,17},{17,25},{2,10},{10,18},{18,26},{... | collective-permute-start | bytes 706568 | tf_op jit(solution)/shard_map/while/body/eval_jaxpr/ppermute | solution.py:14
  687.6 0.9 copy-start.2
  687.6 0.9 copy-start.3
where the time goes:
time: 692 us; the launch traced here: 689 us
  blocking collectives  296 us (43%)
  starting transfers between devices  145 us (21%)
  local copies, waits for them, and re-layouts  109 us (16%)
  other arithmetic  68.2 us (10%)
  waiting for transfers between devices  30.8 us (4%)
  loops' own time  25.7 us (4%)
  matrix products  12.9 us (2%)
    all_gather x7, blocking collectives, window_work(): all_coeffs = lax.all_gather(beta_prior, 'obs', axis=2, tiled=True)  173 us
    psum x7, blocking collectives, window_work(): totals = lax.psum(statistics, 'obs')  123 us
    ppermute x7, starting transfers between devices, from_behind(): return lax.ppermute(array, axis, pairs)  95 us
    dynamic_update_slice x28, local copies, waits for them, and re-layouts, store_entry(): return lax.dynamic_update_slice_in_dim(buffer, updated, slot_index, 1)  43.8 us
    all_to_all x7, waiting for transfers between devices, window_work(): lax.all_to_all(send_rows, 'obs', split_axis=1, concat_axis=1, tiled=True)  30.8 us
    all_to_all x7, starting transfers between devices, window_work(): lax.all_to_all(send_channel, 'obs', split_axis=1, concat_axis=1, tiled=True)  26.2 us
    another operation x1, loops' own time, local(): lax.fori_loop(0, stream_count + section_count - 1, tick_step, initial)  25.7 us
    all_to_all x7, starting transfers between devices, window_work(): lax.all_to_all(send_rows, 'obs', split_axis=1, concat_axis=1, tiled=True)  23.5 us
  transfers between devices with their start and end apart: 21, of which 7 were waited for; matrix products, arithmetic and copies ran while one was open for 18% of the time, Pallas kernels for 0%

commit v1 on v0

--- a/solution.py
+++ b/solution.py
@@ -1,3 +1,4 @@
+import functools
 import jax
 import jax.numpy as jnp
 import numpy as np
@@ -6,6 +7,19 @@
 
 HUBER_SQ = 9.0
 PRIOR_WEIGHT = 64.0
+
+
+def _refer_chains(frame, named_axis):
+    right_arr = lax.all_to_all(
+        jnp.stack(jnp.split(frame, lax.axis_size(named_axis), axis=1)),
+        axis_name=named_axis,
+        split_axis=0,
+        concat_axis=0,
+    )
+    return jnp.concatenate(right_arr, axis=1)
+
+
+define_things_all = functools.partial(_refer_chains, named_axis="obs")
 
 
 def from_behind(array, axis, by):
@@ -156,7 +170,7 @@
         totals = lax.psum(statistics, "obs")
         send_rows, send_channel = jax.vmap(pack_blocks)(block_sums, channel)
         got_rows, got_channel = (
-            lax.all_to_all(send_rows, "obs", split_axis=1, concat_axis=1, tiled=True),
+            define_things_all(send_rows),
             lax.all_to_all(send_channel, "obs", split_axis=1, concat_axis=1, tiled=True),
         )
         normal = jax.vmap(unpack_blocks)(got_rows, got_channel)

time: 692 us -> 721 us (1.042)
  local copies, waits for them, and re-layouts: 109 us -> 143 us
    while x42 -> x91, local copies, waits for them, and re-layouts: 9.87 us -> 39.2 us
  transfers between devices with their start and end apart: 21 -> 21, of which waited for: 7 -> 7; matrix products, arithmetic and copies ran while one was open for 18% -> 22% of each run, Pallas kernels for 0% -> 0%
where the time goes in v1:
time: 721 us; the launch traced here: 718 us
  blocking collectives  296 us (41%)
  starting transfers between devices  145 us (20%)
  local copies, waits for them, and re-layouts  143 us (20%)
  other arithmetic  68.1 us (9%)
  waiting for transfers between devices  30.9 us (4%)
  loops' own time  25.8 us (4%)
  matrix products  8.5 us (1%)
    all_gather x7, blocking collectives, window_work(): all_coeffs = lax.all_gather(beta_prior, 'obs', axis=2, tiled=True)  173 us
    psum x7, blocking collectives, window_work(): totals = lax.psum(statistics, 'obs')  123 us
    ppermute x7, starting transfers between devices, from_behind(): return lax.ppermute(array, axis, pairs)  94.9 us
    dynamic_update_slice x28, local copies, waits for them, and re-layouts, store_entry(): return lax.dynamic_update_slice_in_dim(buffer, updated, slot_index, 1)  43.8 us
    while x91, local copies, waits for them, and re-layouts  39.2 us
    all_to_all x7, waiting for transfers between devices, _refer_chains(): lax.all_to_all(jnp.stack(jnp.split(frame, lax.axis_size(named_axis), axis...  30.9 us
    all_to_all x7, starting transfers between devices, window_work(): lax.all_to_all(send_channel, 'obs', split_axis=1, concat_axis=1, tiled=True)  26.2 us
    another operation x1, loops' own time, local(): lax.fori_loop(0, stream_count + section_count - 1, tick_step, initial)  25.8 us
  transfers between devices with their start and end apart: 21, of which 7 were waited for; matrix products, arithmetic and copies ran while one was open for 22% of the time, Pallas kernels for 0%

profile of v1, /device:TPU:1, one launch (start us, length us, event | category | flops | bytes accessed | tf_op | source)
XLA Modules:
  0.0 717.6 jit_solution(7892731832164856069)
XLA Ops:
  0.6 1.5 copy.674
  2.9 713.8 %while.38 = (s32[]{:T(128)}, f32[1,230,256]{2,1,0:T(8,128)S(1)}, f32[1,4,20,256]{3,1,2,0:T(4,128)S(1)}, f32[1,4,210,256]{3,1,2,0:T(4,128)S(1)}, s32[]{:T(128)}, ...) while((s32[]{:T(128)}, f32[1,230,256]{2,1,0:T(8,128)S(1)}, ...), condition=%wide.region_8.10_spmd.clone.clone, body=%wide.region_0.9_spmd.sunk.clone.clone.sunk | while | flops 57759508 | bytes 13978125 | solution.py:213
  7.5 6.4 all-to-all-start.1
  13.9 1.4 constant_dynamic-slice_fusion.10
  16.3 24.6 %all_gather.15 = f32[1,20,2048]{2,1,0:T(8,128)S(1)} all-gather(f32[1,20,256]{2,1,0:T(8,128)S(1)} %slice.5342), channel_id=1, replica_groups=mesh['section'=4,'obs'=8] {'obs'}, dimensions={2}, use_global_device_ids=true | all-gather | bytes 184320 | tf_op jit(solution)/shard_map/while/body/eval_jaxpr/all_gather | solution.py:158
  42.3 1.6 fusion.473
  52.6 17.5 %psum.19 = f32[1,2]{1,0:T(1,128)S(1)} all-reduce(f32[1,2]{1,0:T(1,128)S(1)} %maximum_bitcast_fusion.6), channel_id=1, replica_groups=mesh['section'=4,'obs'=8] {'obs'}, use_global_device_ids=true, to_apply=%region_7.8 | all-reduce | flops 2 | bytes 16 | tf_op jit(solution)/shard_map/while/body/eval_jaxpr/psum | solution.py:170
  72.1 3.4 all-to-all-start
  76.8 4.4 all-to-all-done
  87.4 15.6 %collective-permute-start = (f32[1,230,256]{2,1,0:T(8,128)S(1)}, f32[1,230,256]{2,1,0:T(8,128)S(1)}, u32[]{:S(2)}, u32[]{:S(2)}) collective-permute-start(f32[1,230,256]{2,1,0:T(8,128)S(1)} %pad_maximum_fusion.2), channel_id=1, source_target_pairs={{0,8},{8,16},{16,24},{1,9},{9,17},{17,25},{2,10},{10,18},{18,26},{... | collective-permute-start | bytes 706568 | tf_op jit(solution)/shard_map/while/body/eval_jaxpr/ppermute | solution.py:28
  103.4 5.9 dynamic_update_slice.31
  113.9 3.3 all-to-all-start.1
  117.3 1.4 constant_dynamic-slice_fusion.10
  119.7 25.2 %all_gather.15 = f32[1,20,2048]{2,1,0:T(8,128)S(1)} all-gather(f32[1,20,256]{2,1,0:T(8,128)S(1)} %slice.5342), channel_id=1, replica_groups=mesh['section'=4,'obs'=8] {'obs'}, dimensions={2}, use_global_device_ids=true | all-gather | bytes 184320 | tf_op jit(solution)/shard_map/while/body/eval_jaxpr/all_gather | solution.py:158
  146.3 1.6 fusion.473
  156.6 17.3 %psum.19 = f32[1,2]{1,0:T(1,128)S(1)} all-reduce(f32[1,2]{1,0:T(1,128)S(1)} %maximum_bitcast_fusion.6), channel_id=1, replica_groups=mesh['section'=4,'obs'=8] {'obs'}, use_global_device_ids=true, to_apply=%region_7.8 | all-reduce | flops 2 | bytes 16 | tf_op jit(solution)/shard_map/while/body/eval_jaxpr/psum | solution.py:170
  175.9 3.4 all-to-all-start
  180.6 4.4 all-to-all-done
  191.2 13.1 %collective-permute-start = (f32[1,230,256]{2,1,0:T(8,128)S(1)}, f32[1,230,256]{2,1,0:T(8,128)S(1)}, u32[]{:S(2)}, u32[]{:S(2)}) collective-permute-start(f32[1,230,256]{2,1,0:T(8,128)S(1)} %pad_maximum_fusion.2), channel_id=1, source_target_pairs={{0,8},{8,16},{16,24},{1,9},{9,17},{17,25},{2,10},{10,18},{18,26},{... | collective-permute-start | bytes 706568 | tf_op jit(solution)/shard_map/while/body/eval_jaxpr/ppermute | solution.py:28
  204.6 5.9 dynamic_update_slice.31
  215.2 3.3 all-to-all-start.1
  218.5 1.4 constant_dynamic-slice_fusion.10
  220.9 24.6 %all_gather.15 = f32[1,20,2048]{2,1,0:T(8,128)S(1)} all-gather(f32[1,20,256]{2,1,0:T(8,128)S(1)} %slice.5342), channel_id=1, replica_groups=mesh['section'=4,'obs'=8] {'obs'}, dimensions={2}, use_global_device_ids=true | all-gather | bytes 184320 | tf_op jit(solution)/shard_map/while/body/eval_jaxpr/all_gather | solution.py:158
  247.0 1.6 fusion.473
  257.3 17.5 %psum.19 = f32[1,2]{1,0:T(1,128)S(1)} all-reduce(f32[1,2]{1,0:T(1,128)S(1)} %maximum_bitcast_fusion.6), channel_id=1, replica_groups=mesh['section'=4,'obs'=8] {'obs'}, use_global_device_ids=true, to_apply=%region_7.8 | all-reduce | flops 2 | bytes 16 | tf_op jit(solution)/shard_map/while/body/eval_jaxpr/psum | solution.py:170
  276.8 3.4 all-to-all-start
  281.5 4.4 all-to-all-done
  292.1 13.4 %collective-permute-start = (f32[1,230,256]{2,1,0:T(8,128)S(1)}, f32[1,230,256]{2,1,0:T(8,128)S(1)}, u32[]{:S(2)}, u32[]{:S(2)}) collective-permute-start(f32[1,230,256]{2,1,0:T(8,128)S(1)} %pad_maximum_fusion.2), channel_id=1, source_target_pairs={{0,8},{8,16},{16,24},{1,9},{9,17},{17,25},{2,10},{10,18},{18,26},{... | collective-permute-start | bytes 706568 | tf_op jit(solution)/shard_map/while/body/eval_jaxpr/ppermute | solution.py:28
  305.9 5.9 dynamic_update_slice.31
  316.4 3.3 all-to-all-start.1
  319.7 1.4 constant_dynamic-slice_fusion.10
  322.1 24.8 %all_gather.15 = f32[1,20,2048]{2,1,0:T(8,128)S(1)} all-gather(f32[1,20,256]{2,1,0:T(8,128)S(1)} %slice.5342), channel_id=1, replica_groups=mesh['section'=4,'obs'=8] {'obs'}, dimensions={2}, use_global_device_ids=true | all-gather | bytes 184320 | tf_op jit(solution)/shard_map/while/body/eval_jaxpr/all_gather | solution.py:158
  348.5 1.6 fusion.473
  358.7 17.6 %psum.19 = f32[1,2]{1,0:T(1,128)S(1)} all-reduce(f32[1,2]{1,0:T(1,128)S(1)} %maximum_bitcast_fusion.6), channel_id=1, replica_groups=mesh['section'=4,'obs'=8] {'obs'}, use_global_device_ids=true, to_apply=%region_7.8 | all-reduce | flops 2 | bytes 16 | tf_op jit(solution)/shard_map/while/body/eval_jaxpr/psum | solution.py:170
  378.4 3.4 all-to-all-start
  383.0 4.4 all-to-all-done
  393.6 13.1 %collective-permute-start = (f32[1,230,256]{2,1,0:T(8,128)S(1)}, f32[1,230,256]{2,1,0:T(8,128)S(1)}, u32[]{:S(2)}, u32[]{:S(2)}) collective-permute-start(f32[1,230,256]{2,1,0:T(8,128)S(1)} %pad_maximum_fusion.2), channel_id=1, source_target_pairs={{0,8},{8,16},{16,24},{1,9},{9,17},{17,25},{2,10},{10,18},{18,26},{... | collective-permute-start | bytes 706568 | tf_op jit(solution)/shard_map/while/body/eval_jaxpr/ppermute | solution.py:28
  407.1 5.9 dynamic_update_slice.31
  417.6 3.3 all-to-all-start.1
  423.4 24.9 %all_gather.15 = f32[1,20,2048]{2,1,0:T(8,128)S(1)} all-gather(f32[1,20,256]{2,1,0:T(8,128)S(1)} %slice.5342), channel_id=1, replica_groups=mesh['section'=4,'obs'=8] {'obs'}, dimensions={2}, use_global_device_ids=true | all-gather | bytes 184320 | tf_op jit(solution)/shard_map/while/body/eval_jaxpr/all_gather | solution.py:158
  449.8 1.6 fusion.473
  460.1 17.2 %psum.19 = f32[1,2]{1,0:T(1,128)S(1)} all-reduce(f32[1,2]{1,0:T(1,128)S(1)} %maximum_bitcast_fusion.6), channel_id=1, replica_groups=mesh['section'=4,'obs'=8] {'obs'}, use_global_device_ids=true, to_apply=%region_7.8 | all-reduce | flops 2 | bytes 16 | tf_op jit(solution)/shard_map/while/body/eval_jaxpr/psum | solution.py:170
  479.3 3.4 all-to-all-start
  483.9 4.4 all-to-all-done
  494.5 13.4 %collective-permute-start = (f32[1,230,256]{2,1,0:T(8,128)S(1)}, f32[1,230,256]{2,1,0:T(8,128)S(1)}, u32[]{:S(2)}, u32[]{:S(2)}) collective-permute-start(f32[1,230,256]{2,1,0:T(8,128)S(1)} %pad_maximum_fusion.2), channel_id=1, source_target_pairs={{0,8},{8,16},{16,24},{1,9},{9,17},{17,25},{2,10},{10,18},{18,26},{... | collective-permute-start | bytes 706568 | tf_op jit(solution)/shard_map/while/body/eval_jaxpr/ppermute | solution.py:28
  508.3 5.9 dynamic_update_slice.31
  518.9 3.3 all-to-all-start.1
  522.2 1.4 constant_dynamic-slice_fusion.10
  524.6 24.8 %all_gather.15 = f32[1,20,2048]{2,1,0:T(8,128)S(1)} all-gather(f32[1,20,256]{2,1,0:T(8,128)S(1)} %slice.5342), channel_id=1, replica_groups=mesh['section'=4,'obs'=8] {'obs'}, dimensions={2}, use_global_device_ids=true | all-gather | bytes 184320 | tf_op jit(solution)/shard_map/while/body/eval_jaxpr/all_gather | solution.py:158
  550.9 1.6 fusion.473
  561.2 17.5 %psum.19 = f32[1,2]{1,0:T(1,128)S(1)} all-reduce(f32[1,2]{1,0:T(1,128)S(1)} %maximum_bitcast_fusion.6), channel_id=1, replica_groups=mesh['section'=4,'obs'=8] {'obs'}, use_global_device_ids=true, to_apply=%region_7.8 | all-reduce | flops 2 | bytes 16 | tf_op jit(solution)/shard_map/while/body/eval_jaxpr/psum | solution.py:170
  580.7 3.4 all-to-all-start
  585.4 4.4 all-to-all-done
  596.0 13.2 %collective-permute-start = (f32[1,230,256]{2,1,0:T(8,128)S(1)}, f32[1,230,256]{2,1,0:T(8,128)S(1)}, u32[]{:S(2)}, u32[]{:S(2)}) collective-permute-start(f32[1,230,256]{2,1,0:T(8,128)S(1)} %pad_maximum_fusion.2), channel_id=1, source_target_pairs={{0,8},{8,16},{16,24},{1,9},{9,17},{17,25},{2,10},{10,18},{18,26},{... | collective-permute-start | bytes 706568 | tf_op jit(solution)/shard_map/while/body/eval_jaxpr/ppermute | solution.py:28
  609.6 5.9 dynamic_update_slice.31
  620.1 3.3 all-to-all-start.1
  623.4 1.4 constant_dynamic-slice_fusion.10
  625.8 24.5 %all_gather.15 = f32[1,20,2048]{2,1,0:T(8,128)S(1)} all-gather(f32[1,20,256]{2,1,0:T(8,128)S(1)} %slice.5342), channel_id=1, replica_groups=mesh['section'=4,'obs'=8] {'obs'}, dimensions={2}, use_global_device_ids=true | all-gather | bytes 184320 | tf_op jit(solution)/shard_map/while/body/eval_jaxpr/all_gather | solution.py:158
  651.8 1.6 fusion.473
  662.0 18.0 %psum.19 = f32[1,2]{1,0:T(1,128)S(1)} all-reduce(f32[1,2]{1,0:T(1,128)S(1)} %maximum_bitcast_fusion.6), channel_id=1, replica_groups=mesh['section'=4,'obs'=8] {'obs'}, use_global_device_ids=true, to_apply=%region_7.8 | all-reduce | flops 2 | bytes 16 | tf_op jit(solution)/shard_map/while/body/eval_jaxpr/psum | solution.py:170
  682.1 3.4 all-to-all-start
  686.7 4.4 all-to-all-done
  697.3 13.1 %collective-permute-start = (f32[1,230,256]{2,1,0:T(8,128)S(1)}, f32[1,230,256]{2,1,0:T(8,128)S(1)}, u32[]{:S(2)}, u32[]{:S(2)}) collective-permute-start(f32[1,230,256]{2,1,0:T(8,128)S(1)} %pad_maximum_fusion.2), channel_id=1, source_target_pairs={{0,8},{8,16},{16,24},{1,9},{9,17},{17,25},{2,10},{10,18},{18,26},{... | collective-permute-start | bytes 706568 | tf_op jit(solution)/shard_map/while/body/eval_jaxpr/ppermute | solution.py:28
  710.8 5.9 dynamic_update_slice.31
  (672 shorter events, 157.3 us)
Async XLA Ops:
  2.2 0.7 copy-start.4
  2.3 0.7 copy-start.5
  2.3 0.7 copy-start.6
  7.5 64.6 %all-to-all-start.1 = ((f32[1,8,8]{2,0,1:T(1,128)}), f32[1,8,8]{2,0,1:T(1,128)S(1)}, u32[]{:S(2)}, u32[]{:S(2)}) async-start(f32[1,8,8]{2,0,1:T(1,128)} %bitcast.2500), calls=%async_computation.1 | async-start | bytes 8192 | tf_op jit(solution)/shard_map/while/body/eval_jaxpr/all_to_all | solution.py:174
  72.1 9.1 %all-to-all-start = ((f32[8,1,1,8,230]{4,3,2,1,0:T(8,128)}), f32[8,1,1,8,230]{4,3,2,1,0:T(8,128)S(1)}, u32[]{:S(2)}, u32[]{:S(2)}) async-start(f32[8,1,1,8,230]{4,3,2,1,0:T(8,128)} %constant_dynamic-update-slice_fusion.23), calls=%async_computation | async-start | bytes 131072 | tf_op jit(solution)/shard_map/while/body/eval_jaxpr/all_to_all | solution.py:13
  81.6 0.6 copy-start
  83.0 0.7 slice-start
  84.9 0.7 copy-start.1
  87.4 21.9 %collective-permute-start = (f32[1,230,256]{2,1,0:T(8,128)S(1)}, f32[1,230,256]{2,1,0:T(8,128)S(1)}, u32[]{:S(2)}, u32[]{:S(2)}) collective-permute-start(f32[1,230,256]{2,1,0:T(8,128)S(1)} %pad_maximum_fusion.2), channel_id=1, source_target_pairs={{0,8},{8,16},{16,24},{1,9},{9,17},{17,25},{2,10},{10,18},{18,26},{... | collective-permute-start | bytes 706568 | tf_op jit(solution)/shard_map/while/body/eval_jaxpr/ppermute | solution.py:28
  113.9 62.0 %all-to-all-start.1 = ((f32[1,8,8]{2,0,1:T(1,128)}), f32[1,8,8]{2,0,1:T(1,128)S(1)}, u32[]{:S(2)}, u32[]{:S(2)}) async-start(f32[1,8,8]{2,0,1:T(1,128)} %bitcast.2500), calls=%async_computation.1 | async-start | bytes 8192 | tf_op jit(solution)/shard_map/while/body/eval_jaxpr/all_to_all | solution.py:174
  175.9 9.1 %all-to-all-start = ((f32[8,1,1,8,230]{4,3,2,1,0:T(8,128)}), f32[8,1,1,8,230]{4,3,2,1,0:T(8,128)S(1)}, u32[]{:S(2)}, u32[]{:S(2)}) async-start(f32[8,1,1,8,230]{4,3,2,1,0:T(8,128)} %constant_dynamic-update-slice_fusion.23), calls=%async_computation | async-start | bytes 131072 | tf_op jit(solution)/shard_map/while/body/eval_jaxpr/all_to_all | solution.py:13
  185.4 0.6 copy-start
  186.8 0.7 slice-start
  188.7 0.7 copy-start.1
  191.2 19.4 %collective-permute-start = (f32[1,230,256]{2,1,0:T(8,128)S(1)}, f32[1,230,256]{2,1,0:T(8,128)S(1)}, u32[]{:S(2)}, u32[]{:S(2)}) collective-permute-start(f32[1,230,256]{2,1,0:T(8,128)S(1)} %pad_maximum_fusion.2), channel_id=1, source_target_pairs={{0,8},{8,16},{16,24},{1,9},{9,17},{17,25},{2,10},{10,18},{18,26},{... | collective-permute-start | bytes 706568 | tf_op jit(solution)/shard_map/while/body/eval_jaxpr/ppermute | solution.py:28
  215.2 61.7 %all-to-all-start.1 = ((f32[1,8,8]{2,0,1:T(1,128)}), f32[1,8,8]{2,0,1:T(1,128)S(1)}, u32[]{:S(2)}, u32[]{:S(2)}) async-start(f32[1,8,8]{2,0,1:T(1,128)} %bitcast.2500), calls=%async_computation.1 | async-start | bytes 8192 | tf_op jit(solution)/shard_map/while/body/eval_jaxpr/all_to_all | solution.py:174
  276.8 9.1 %all-to-all-start = ((f32[8,1,1,8,230]{4,3,2,1,0:T(8,128)}), f32[8,1,1,8,230]{4,3,2,1,0:T(8,128)S(1)}, u32[]{:S(2)}, u32[]{:S(2)}) async-start(f32[8,1,1,8,230]{4,3,2,1,0:T(8,128)} %constant_dynamic-update-slice_fusion.23), calls=%async_computation | async-start | bytes 131072 | tf_op jit(solution)/shard_map/while/body/eval_jaxpr/all_to_all | solution.py:13
  286.3 0.6 copy-start
  287.7 0.7 slice-start
  289.6 0.7 copy-start.1
  292.1 19.7 %collective-permute-start = (f32[1,230,256]{2,1,0:T(8,128)S(1)}, f32[1,230,256]{2,1,0:T(8,128)S(1)}, u32[]{:S(2)}, u32[]{:S(2)}) collective-permute-start(f32[1,230,256]{2,1,0:T(8,128)S(1)} %pad_maximum_fusion.2), channel_id=1, source_target_pairs={{0,8},{8,16},{16,24},{1,9},{9,17},{17,25},{2,10},{10,18},{18,26},{... | collective-permute-start | bytes 706568 | tf_op jit(solution)/shard_map/while/body/eval_jaxpr/ppermute | solution.py:28
  316.4 62.0 %all-to-all-start.1 = ((f32[1,8,8]{2,0,1:T(1,128)}), f32[1,8,8]{2,0,1:T(1,128)S(1)}, u32[]{:S(2)}, u32[]{:S(2)}) async-start(f32[1,8,8]{2,0,1:T(1,128)} %bitcast.2500), calls=%async_computation.1 | async-start | bytes 8192 | tf_op jit(solution)/shard_map/while/body/eval_jaxpr/all_to_all | solution.py:174
  378.4 9.1 %all-to-all-start = ((f32[8,1,1,8,230]{4,3,2,1,0:T(8,128)}), f32[8,1,1,8,230]{4,3,2,1,0:T(8,128)S(1)}, u32[]{:S(2)}, u32[]{:S(2)}) async-start(f32[8,1,1,8,230]{4,3,2,1,0:T(8,128)} %constant_dynamic-update-slice_fusion.23), calls=%async_computation | async-start | bytes 131072 | tf_op jit(solution)/shard_map/while/body/eval_jaxpr/all_to_all | solution.py:13
  387.8 0.6 copy-start
  389.2 0.7 slice-start
  391.2 0.7 copy-start.1
  393.6 19.4 %collective-permute-start = (f32[1,230,256]{2,1,0:T(8,128)S(1)}, f32[1,230,256]{2,1,0:T(8,128)S(1)}, u32[]{:S(2)}, u32[]{:S(2)}) collective-permute-start(f32[1,230,256]{2,1,0:T(8,128)S(1)} %pad_maximum_fusion.2), channel_id=1, source_target_pairs={{0,8},{8,16},{16,24},{1,9},{9,17},{17,25},{2,10},{10,18},{18,26},{... | collective-permute-start | bytes 706568 | tf_op jit(solution)/shard_map/while/body/eval_jaxpr/ppermute | solution.py:28
  417.6 61.7 %all-to-all-start.1 = ((f32[1,8,8]{2,0,1:T(1,128)}), f32[1,8,8]{2,0,1:T(1,128)S(1)}, u32[]{:S(2)}, u32[]{:S(2)}) async-start(f32[1,8,8]{2,0,1:T(1,128)} %bitcast.2500), calls=%async_computation.1 | async-start | bytes 8192 | tf_op jit(solution)/shard_map/while/body/eval_jaxpr/all_to_all | solution.py:174
  479.3 9.1 %all-to-all-start = ((f32[8,1,1,8,230]{4,3,2,1,0:T(8,128)}), f32[8,1,1,8,230]{4,3,2,1,0:T(8,128)S(1)}, u32[]{:S(2)}, u32[]{:S(2)}) async-start(f32[8,1,1,8,230]{4,3,2,1,0:T(8,128)} %constant_dynamic-update-slice_fusion.23), calls=%async_computation | async-start | bytes 131072 | tf_op jit(solution)/shard_map/while/body/eval_jaxpr/all_to_all | solution.py:13
  488.7 0.6 copy-start
  490.1 0.7 slice-start
  492.1 0.7 copy-start.1
  494.5 19.7 %collective-permute-start = (f32[1,230,256]{2,1,0:T(8,128)S(1)}, f32[1,230,256]{2,1,0:T(8,128)S(1)}, u32[]{:S(2)}, u32[]{:S(2)}) collective-permute-start(f32[1,230,256]{2,1,0:T(8,128)S(1)} %pad_maximum_fusion.2), channel_id=1, source_target_pairs={{0,8},{8,16},{16,24},{1,9},{9,17},{17,25},{2,10},{10,18},{18,26},{... | collective-permute-start | bytes 706568 | tf_op jit(solution)/shard_map/while/body/eval_jaxpr/ppermute | solution.py:28
  518.9 61.9 %all-to-all-start.1 = ((f32[1,8,8]{2,0,1:T(1,128)}), f32[1,8,8]{2,0,1:T(1,128)S(1)}, u32[]{:S(2)}, u32[]{:S(2)}) async-start(f32[1,8,8]{2,0,1:T(1,128)} %bitcast.2500), calls=%async_computation.1 | async-start | bytes 8192 | tf_op jit(solution)/shard_map/while/body/eval_jaxpr/all_to_all | solution.py:174
  580.7 9.1 %all-to-all-start = ((f32[8,1,1,8,230]{4,3,2,1,0:T(8,128)}), f32[8,1,1,8,230]{4,3,2,1,0:T(8,128)S(1)}, u32[]{:S(2)}, u32[]{:S(2)}) async-start(f32[8,1,1,8,230]{4,3,2,1,0:T(8,128)} %constant_dynamic-update-slice_fusion.23), calls=%async_computation | async-start | bytes 131072 | tf_op jit(solution)/shard_map/while/body/eval_jaxpr/all_to_all | solution.py:13
  590.2 0.6 copy-start
  591.6 0.7 slice-start
  593.5 0.7 copy-start.1
  596.0 19.5 %collective-permute-start = (f32[1,230,256]{2,1,0:T(8,128)S(1)}, f32[1,230,256]{2,1,0:T(8,128)S(1)}, u32[]{:S(2)}, u32[]{:S(2)}) collective-permute-start(f32[1,230,256]{2,1,0:T(8,128)S(1)} %pad_maximum_fusion.2), channel_id=1, source_target_pairs={{0,8},{8,16},{16,24},{1,9},{9,17},{17,25},{2,10},{10,18},{18,26},{... | collective-permute-start | bytes 706568 | tf_op jit(solution)/shard_map/while/body/eval_jaxpr/ppermute | solution.py:28
  620.1 62.0 %all-to-all-start.1 = ((f32[1,8,8]{2,0,1:T(1,128)}), f32[1,8,8]{2,0,1:T(1,128)S(1)}, u32[]{:S(2)}, u32[]{:S(2)}) async-start(f32[1,8,8]{2,0,1:T(1,128)} %bitcast.2500), calls=%async_computation.1 | async-start | bytes 8192 | tf_op jit(solution)/shard_map/while/body/eval_jaxpr/all_to_all | solution.py:174
  682.1 9.1 %all-to-all-start = ((f32[8,1,1,8,230]{4,3,2,1,0:T(8,128)}), f32[8,1,1,8,230]{4,3,2,1,0:T(8,128)S(1)}, u32[]{:S(2)}, u32[]{:S(2)}) async-start(f32[8,1,1,8,230]{4,3,2,1,0:T(8,128)} %constant_dynamic-update-slice_fusion.23), calls=%async_computation | async-start | bytes 131072 | tf_op jit(solution)/shard_map/while/body/eval_jaxpr/all_to_all | solution.py:13
  691.5 0.6 copy-start
  692.9 0.7 slice-start
  694.8 0.7 copy-start.1
  697.3 19.4 %collective-permute-start = (f32[1,230,256]{2,1,0:T(8,128)S(1)}, f32[1,230,256]{2,1,0:T(8,128)S(1)}, u32[]{:S(2)}, u32[]{:S(2)}) collective-permute-start(f32[1,230,256]{2,1,0:T(8,128)S(1)} %pad_maximum_fusion.2), channel_id=1, source_target_pairs={{0,8},{8,16},{16,24},{1,9},{9,17},{17,25},{2,10},{10,18},{18,26},{... | collective-permute-start | bytes 706568 | tf_op jit(solution)/shard_map/while/body/eval_jaxpr/ppermute | solution.py:28
  716.7 0.9 copy-start.2
  716.7 0.9 copy-start.3
